TPU v7x, 32 devices: a whole 2x2x4 slice. The times are simulated.
32 devices in a mesh: head: 2 (over x), tok: 16 (over z, y, core).
Axes of the slice: x: 2, y: 2, z: 4, core: 2. Of those that a mesh axis runs over, the one named last changes fastest.
Arguments:
- queries: bfloat16 [3072, 1024], P('tok', 'head'), may hold values from -512 to 512
- keys: bfloat16 [3072, 1024], P('tok', 'head'), may hold values from -8 to 8
- values: bfloat16 [3072, 1024], P('tok', 'head'), may hold values from -6 to 6
- out_grad: bfloat16 [3072, 1024], P('tok', 'head'), may hold values from -6 to 6
- w_query: bfloat16 [1024, 1024], P(None, 'head'), may hold values from -0.1875 to 0.1875
- w_key: bfloat16 [1024, 1024], P(None, 'head'), may hold values from -0.1875 to 0.1875
- w_value: bfloat16 [1024, 1024], P(None, 'head'), may hold values from -0.1875 to 0.1875
- w_out: bfloat16 [1024, 1024], P('head'), may hold values from -0.1875 to 0.1875
- page_cluster: int32 [96], replicated, may hold values from 0 to 15, as said below
Outputs:
- input_grad: bfloat16 [3072, 1024], P('tok', 'head')
Inputs may be any that keep to these rules, and one draw needn't show every extreme that they name: `page_cluster`: the 6 pages k * 6 to k * 6 + 5, for each k, name distinct clusters. No cluster is named by more than 8 pages, and some cluster by exactly 8.
All inputs are finite; a program needn't handle non-finite values.
Results may differ from a plain program's by a relative error of at most 0.014.
Values may be sent and summed in bfloat16 or wider, within the bound.
A program may use at most 64 MiB of HBM per device.

v0:
```python
import jax
import jax.numpy as jnp
from jax import lax
from jax.sharding import PartitionSpec as P

HEAD_DIM = 128
PAGE = 32


def per_device(queries, keys, values, out_grad, w_query, w_key, w_value, w_out, page_cluster):
    tok_rows, head_cols = queries.shape
    pages_here = tok_rows // PAGE
    heads_here = head_cols // HEAD_DIM
    peers = lax.axis_size("tok")
    myself = lax.axis_index("tok")
    page_total = page_cluster.shape[0]
    slot_count = peers // 2
    cluster_rows = slot_count * PAGE
    score_scale = HEAD_DIM ** (-0.5)
    grad_heads = jnp.einsum(
        "td,hd->th",
        lax.all_gather(out_grad, "head", axis=1, tiled=True),
        w_out,
        preferred_element_type=jnp.float32,
    ).astype(jnp.bfloat16)
    page_order = jnp.arange(page_total, dtype=jnp.int32)
    peer_order = jnp.arange(peers, dtype=jnp.int32)
    cluster_onehot = (page_cluster[:, None] == peer_order[None, :]).astype(jnp.int32)
    running_count = jnp.cumsum(cluster_onehot, axis=0) - cluster_onehot
    page_rank = jnp.sum(running_count * cluster_onehot, axis=1)
    my_clusters = lax.dynamic_slice_in_dim(page_cluster, myself * pages_here, pages_here)
    going = my_clusters[None, :] == peer_order[:, None]
    going_any = jnp.any(going, axis=1)
    going_index = jnp.sum(
        going.astype(jnp.int32) * jnp.arange(pages_here, dtype=jnp.int32)[None, :], axis=1
    )

    def outgoing(matrix):
        paged = matrix.reshape(pages_here, PAGE, matrix.shape[1])
        picked = jnp.take(paged, going_index, axis=0)
        return jnp.where(going_any[:, None, None], picked, jnp.zeros_like(picked))

    arrived = (
        lax.all_to_all(outgoing(queries), "tok", split_axis=0, concat_axis=0, tiled=True),
        lax.all_to_all(outgoing(keys), "tok", split_axis=0, concat_axis=0, tiled=True),
        lax.all_to_all(outgoing(values), "tok", split_axis=0, concat_axis=0, tiled=True),
        lax.all_to_all(outgoing(grad_heads), "tok", split_axis=0, concat_axis=0, tiled=True),
    )
    slot_order = jnp.arange(slot_count, dtype=jnp.int32)
    slot_hit = (page_cluster[None, :] == myself) & (page_rank[None, :] == slot_order[:, None])
    filled = jnp.any(slot_hit, axis=1)
    slot_page = jnp.sum(slot_hit.astype(jnp.int32) * page_order[None, :], axis=1)
    slot_source = slot_page // pages_here

    def assemble(matrix):
        picked = jnp.take(matrix, slot_source, axis=0)
        picked = jnp.where(filled[:, None, None], picked, jnp.zeros_like(picked))
        return picked.reshape(cluster_rows, heads_here, HEAD_DIM)

    slot_query = assemble(arrived[0])
    slot_keys = assemble(arrived[1])
    slot_values = assemble(arrived[2])
    slot_grads = assemble(arrived[3])
    inner_index = jnp.arange(PAGE, dtype=jnp.int32)
    key_pos = (slot_page[:, None] * PAGE + inner_index[None, :]).reshape(cluster_rows)
    key_live = jnp.broadcast_to(filled[:, None], (slot_count, PAGE)).reshape(cluster_rows)
    key_order = jnp.arange(cluster_rows, dtype=jnp.int32)
    block_rows = min(512, cluster_rows)
    dkey_sum = jnp.zeros((cluster_rows, heads_here, HEAD_DIM), jnp.float32)
    dvalue_sum = jnp.zeros((cluster_rows, heads_here, HEAD_DIM), jnp.float32)
    query_parts = []
    for block_index in range(cluster_rows // block_rows):
        first_row = block_index * block_rows
        last_row = first_row + block_rows
        part_query = slot_query[first_row:last_row]
        part_grads = slot_grads[first_row:last_row]
        row_pos = key_pos[first_row:last_row]
        row_order = key_order[first_row:last_row]
        allowed = key_live[None, :] & (key_pos[None, :] <= row_pos[:, None]) | (
            key_order[None, :] == row_order[:, None]
        )
        score = (
            jnp.einsum("qhd,khd->hqk", part_query, slot_keys, preferred_element_type=jnp.float32)
            * score_scale
        )
        score = jnp.where(allowed[None], score, -1e30)
        row_max = jnp.max(score, axis=2, keepdims=True)
        raised = jnp.where(allowed[None], jnp.exp(score - row_max), 0.0)
        weights = raised / jnp.sum(raised, axis=2, keepdims=True)
        weights_half = weights.astype(jnp.bfloat16)
        grad_weights = jnp.einsum(
            "qhd,khd->hqk", part_grads, slot_values, preferred_element_type=jnp.float32
        )
        row_delta = jnp.sum(weights * grad_weights, axis=2, keepdims=True)
        grad_score = (weights * (grad_weights - row_delta)).astype(jnp.bfloat16)
        grad_query = (
            jnp.einsum("hqk,khd->qhd", grad_score, slot_keys, preferred_element_type=jnp.float32)
            * score_scale
        )
        query_parts.append(grad_query.astype(jnp.bfloat16))
        dkey_sum = dkey_sum + jnp.einsum(
            "hqk,qhd->khd", grad_score, part_query, preferred_element_type=jnp.float32
        )
        dvalue_sum = dvalue_sum + jnp.einsum(
            "hqk,qhd->khd", weights_half, part_grads, preferred_element_type=jnp.float32
        )
    slot_dquery = jnp.concatenate(query_parts, axis=0).reshape(cluster_rows, head_cols)
    slot_dkey = (dkey_sum * score_scale).astype(jnp.bfloat16).reshape(cluster_rows, head_cols)
    slot_dvalue = dvalue_sum.astype(jnp.bfloat16).reshape(cluster_rows, head_cols)
    back_hit = (slot_source[None, :] == peer_order[:, None]) & filled[None, :]
    back_any = jnp.any(back_hit, axis=1)
    back_slot = jnp.sum(back_hit.astype(jnp.int32) * slot_order[None, :], axis=1)
    share_rows = w_query.shape[0] // lax.axis_size("head")
    total = jnp.einsum("dh,th->dt", w_query, slot_dquery, preferred_element_type=jnp.float32)
    total = total + jnp.einsum("dh,th->dt", w_key, slot_dkey, preferred_element_type=jnp.float32)
    total = total + jnp.einsum(
        "dh,th->dt", w_value, slot_dvalue, preferred_element_type=jnp.float32
    )
    column_share = lax.psum_scatter(
        total.astype(jnp.bfloat16), "head", scatter_dimension=0, tiled=True
    )
    column_share = column_share.reshape(share_rows, slot_count, PAGE)
    picked = jnp.take(column_share, back_slot, axis=1)
    picked = jnp.where(back_any[None, :, None], picked, jnp.zeros_like(picked))
    returned = lax.all_to_all(picked, "tok", split_axis=1, concat_axis=1, tiled=True)
    input_grad = jnp.take(returned, my_clusters, axis=1).reshape(share_rows, tok_rows).T
    return input_grad


def solution(mesh):
    placed = (
        P("tok", "head"),
        P("tok", "head"),
        P("tok", "head"),
        P("tok", "head"),
        P(None, "head"),
        P(None, "head"),
        P(None, "head"),
        P("head", None),
        P(),
    )
    return jax.shard_map(
        per_device, mesh=mesh, in_specs=placed, out_specs=P("tok", "head"), check_vma=False
    )
```

profile of v0, /device:TPU:0, one launch (start us, length us, event | category | flops | bytes accessed | tf_op | source)
XLA Modules:
  0.0 150.0 jit_solution(11652533963918098453)
XLA Ops:
  6.5 0.8 compare_and_fusion.3
  7.6 8.8 %all_gather.3 = bf16[192,1024]{1,0:T(8,128)(2,1)S(1)} all-gather(bf16[192,512]{1,0:T(8,128)(2,1)} %param.16), channel_id=1, replica_groups=mesh['head'=2,'tok'=16] {'head'}, dimensions={1}, use_global_device_ids=true | all-gather | bytes 589824 | tf_op jit(solution)/shard_map/all_gather | solution.py:22
  16.3 1.8 %convolution_convert_fusion.1 = bf16[192,512]{1,0:T(8,128)(2,1)S(1)} fusion(bf16[192,1024]{1,0:T(8,128)(2,1)S(1)} %all_gather.3, bf16[512,1024]{1,0:T(8,128)(2,1)} %param.20), kind=kOutput, calls=%fused_computation.25 | convolution fusion | flops 201424896 | bytes 1638400 | tf_op jit(solution)/shard_map/td,hd->th/dot_general | solution.py:20
  18.1 0.6 gather_fusion.6
  18.7 0.6 gather_fusion.2
  19.3 0.6 gather_fusion.4
  19.9 0.6 gather_fusion.8
  20.5 1.3 select_select_fusion.2
  21.8 20.2 %all_to_all.25 = bf16[16,32,512]{2,1,0:T(8,128)(2,1)S(1)} all-to-all(bf16[16,32,512]{2,1,0:T(8,128)(2,1)S(1)} %get-tuple-element.18), channel_id=1, replica_groups=mesh['head'=2,'tok'=16] {'tok'}, dimensions={0} | all-to-all | bytes 1048576 | tf_op jit(solution)/shard_map/all_to_all | solution.py:45
  42.0 18.4 %all_to_all.26 = bf16[16,32,512]{2,1,0:T(8,128)(2,1)S(1)} all-to-all(bf16[16,32,512]{2,1,0:T(8,128)(2,1)S(1)} %get-tuple-element.16), channel_id=1, replica_groups=mesh['head'=2,'tok'=16] {'tok'}, dimensions={0} | all-to-all | bytes 1048576 | tf_op jit(solution)/shard_map/all_to_all | solution.py:47
  60.4 4.2 %all-to-all-start.3 = ((bf16[16,32,512]{2,1,0:T(8,128)(2,1)}), bf16[16,32,512]{2,1,0:T(8,128)(2,1)S(1)}, u32[]{:S(2)}, u32[]{:S(2)}) async-start(bf16[16,32,512]{2,1,0:T(8,128)(2,1)} %get-tuple-element.17), calls=%async_computation.3 | async-start | bytes 1048576 | tf_op jit(solution)/shard_map/all_to_all | solution.py:46
  65.4 13.4 %all-to-all-done.3 = bf16[16,32,512]{2,1,0:T(8,128)(2,1)S(1)} async-done(((bf16[16,32,512]{2,1,0:T(8,128)(2,1)}), bf16[16,32,512]{2,1,0:T(8,128)(2,1)S(1)}, u32[]{:S(2)}, u32[]{:S(2)}) %all-to-all-start.3) | async-done | bytes 524320 | tf_op jit(solution)/shard_map/all_to_all | solution.py:46
  78.8 4.2 %all-to-all-start.1 = ((bf16[16,32,512]{2,1,0:T(8,128)(2,1)}), bf16[16,32,512]{2,1,0:T(8,128)(2,1)S(1)}, u32[]{:S(2)}, u32[]{:S(2)}) async-start(bf16[16,32,512]{2,1,0:T(8,128)(2,1)} %get-tuple-element.15), calls=%async_computation.1 | async-start | bytes 1048576 | tf_op jit(solution)/shard_map/all_to_all | solution.py:44
  83.4 0.6 gather_fusion.3
  84.0 0.6 gather_fusion.7
  84.5 0.6 gather_fusion.9
  85.1 12.2 %all-to-all-done.1 = bf16[16,32,512]{2,1,0:T(8,128)(2,1)S(1)} async-done(((bf16[16,32,512]{2,1,0:T(8,128)(2,1)}), bf16[16,32,512]{2,1,0:T(8,128)(2,1)S(1)}, u32[]{:S(2)}, u32[]{:S(2)}) %all-to-all-start.1) | async-done | bytes 524320 | tf_op jit(solution)/shard_map/all_to_all | solution.py:44
  97.3 0.6 gather_fusion.5
  98.9 0.6 fusion.23
  99.5 0.9 convolution_convert_fusion
  101.5 0.5 fusion.24
  101.9 0.7 copy-done.4
  102.7 0.5 convolution_add_fusion.1
  103.2 0.7 copy-done.5
  103.9 1.3 fusion.6
  105.4 14.1 %reduce-scatter.2.cloned.1.call-done = bf16[512,256]{0,1:T(8,128)(2,1)} async-done(((bf16[1024,256]{0,1:T(8,128)(2,1)}), bf16[512,256]{0,1:T(8,128)(2,1)}) %reduce-scatter.2.cloned.1.call-update) | async-done | bytes 262160 | tf_op jit(solution)/shard_map/reduce_scatter | solution.py:119
  119.5 1.5 %gather_fusion = bf16[16,512,32]{1,2,0:T(8,128)(2,1)S(1)} fusion(bf16[512,8,32]{0,2,1:T(8,128)(2,1)} %bitcast.45, s32[1024]{0:T(1024)S(1)} %pad_clamp_fusion.1), kind=kCustom, calls=%fused_computation.8 | custom fusion | bytes 1048640 | tf_op jit(solution)/shard_map/jit(_take)/gather | solution.py:123
  121.0 0.9 select_bitcast_fusion
  122.0 5.6 %all-to-all-start.4 = ((bf16[512,16,32]{0,2,1:T(8,128)(2,1)}), bf16[512,16,32]{0,2,1:T(8,128)(2,1)S(1)}, u32[]{:S(2)}, u32[]{:S(2)}) async-start(bf16[512,16,32]{0,2,1:T(8,128)(2,1)} %select_bitcast_fusion), calls=%async_computation.5 | async-start | bytes 1048576 | tf_op jit(solution)/shard_map/all_to_all | solution.py:125
  127.8 14.1 %all-to-all-done.4 = bf16[512,16,32]{0,2,1:T(8,128)(2,1)S(1)} async-done(((bf16[512,16,32]{0,2,1:T(8,128)(2,1)}), bf16[512,16,32]{0,2,1:T(8,128)(2,1)S(1)}, u32[]{:S(2)}, u32[]{:S(2)}) %all-to-all-start.4) | async-done | bytes 524320 | tf_op jit(solution)/shard_map/all_to_all | solution.py:125
  141.9 0.6 gather_fusion.1
  142.4 0.8 bitcast_select_fusion
  (55 shorter events, 3.8 us)
Async XLA Ops:
  6.5 94.9 %copy-start = (bf16[1024,512]{1,0:T(8,128)(2,1)S(1)}, bf16[1024,512]{1,0:T(8,128)(2,1)}, u32[]{:S(2)}) copy-start(bf16[1024,512]{1,0:T(8,128)(2,1)} %param.17) | copy-start | bytes 3145732
  16.3 2.4 %copy-start.1 = (bf16[192,512]{1,0:T(8,128)(2,1)S(1)}, bf16[192,512]{1,0:T(8,128)(2,1)}, u32[]{:S(2)}) copy-start(bf16[192,512]{1,0:T(8,128)(2,1)} %param.14) | copy-start | bytes 589828
  18.1 1.2 copy-start.2
  18.7 1.2 copy-start.3
  42.0 22.5 %copy-start.6 = (s32[96]{0:T(128)S(1)}, s32[96]{0:T(128)}, u32[]{:S(2)}) copy-start(s32[96]{0:T(128)} %param.21) | copy-start | bytes 1156
  60.4 18.4 %all-to-all-start.3 = ((bf16[16,32,512]{2,1,0:T(8,128)(2,1)}), bf16[16,32,512]{2,1,0:T(8,128)(2,1)S(1)}, u32[]{:S(2)}, u32[]{:S(2)}) async-start(bf16[16,32,512]{2,1,0:T(8,128)(2,1)} %get-tuple-element.17), calls=%async_computation.3 | async-start | bytes 1048576 | tf_op jit(solution)/shard_map/all_to_all | solution.py:46
  78.8 18.4 %all-to-all-start.1 = ((bf16[16,32,512]{2,1,0:T(8,128)(2,1)}), bf16[16,32,512]{2,1,0:T(8,128)(2,1)S(1)}, u32[]{:S(2)}, u32[]{:S(2)}) async-start(bf16[16,32,512]{2,1,0:T(8,128)(2,1)} %get-tuple-element.15), calls=%async_computation.1 | async-start | bytes 1048576 | tf_op jit(solution)/shard_map/all_to_all | solution.py:44
  83.0 36.5 %reduce-scatter.2.cloned.1.call-start = ((), (), s32[]{:S(2)}) async-start(), calls=%async_computation.6 | async-start | bytes 786432 | tf_op jit(solution)/shard_map/reduce_scatter | solution.py:119
  101.4 1.2 copy-start.4
  102.7 1.2 copy-start.5
  122.0 19.9 %all-to-all-start.4 = ((bf16[512,16,32]{0,2,1:T(8,128)(2,1)}), bf16[512,16,32]{0,2,1:T(8,128)(2,1)S(1)}, u32[]{:S(2)}, u32[]{:S(2)}) async-start(bf16[512,16,32]{0,2,1:T(8,128)(2,1)} %select_bitcast_fusion), calls=%async_computation.5 | async-start | bytes 1048576 | tf_op jit(solution)/shard_map/all_to_all | solution.py:125
Sparse Core Ops, SparseCore 0:
  105.3 14.1 reduce-scatter.1
where the time goes:
time: 151 us; the launch traced here: 150 us
  waiting for transfers between devices  53.8 us (36%)
  blocking collectives  47.3 us (31%)
  starting transfers between devices  14 us (9%)
  between operations  13.7 us (9%)
  local copies, waits for them, and re-layouts  9.34 us (6%)
  matrix products  6.38 us (4%)
  other arithmetic  5.46 us (4%)
    all_to_all x1, blocking collectives, per_device(): lax.all_to_all(outgoing(keys), 'tok', split_axis=0, concat_axis=0, tiled=...  20.2 us
    all_to_all x1, blocking collectives, per_device(): lax.all_to_all(outgoing(grad_heads), 'tok', split_axis=0, concat_axis=0,...  18.4 us
    all_to_all x1, waiting for transfers between devices, per_device(): lax.all_to_all(picked, 'tok', split_axis=1, concat_axis=1, tiled=True)  14.1 us
    reduce_scatter x1, waiting for transfers between devices, per_device(): lax.psum_scatter(total.astype(jnp.bfloat16), 'head', scatter_dimension=0,...  14.1 us
    all_to_all x1, waiting for transfers between devices, per_device(): lax.all_to_all(outgoing(values), 'tok', split_axis=0, concat_axis=0, tile...  13.4 us
    all_to_all x1, waiting for transfers between devices, per_device(): lax.all_to_all(outgoing(queries), 'tok', split_axis=0, concat_axis=0, til...  12.2 us
    all_gather x1, blocking collectives, per_device(): lax.all_gather(out_grad, 'head', axis=1, tiled=True)  8.79 us
    all_to_all x1, starting transfers between devices, per_device(): lax.all_to_all(picked, 'tok', split_axis=1, concat_axis=1, tiled=True)  5.62 us
  transfers between devices with their start and end apart: 4, of which 4 were waited for; matrix products, arithmetic and copies ran while one was open for 2% of the time, Pallas kernels for 0%

commit v1 on v0

--- a/solution.py
+++ b/solution.py
@@ -122,7 +122,10 @@
     column_share = column_share.reshape(share_rows, slot_count, PAGE)
     picked = jnp.take(column_share, back_slot, axis=1)
     picked = jnp.where(back_any[None, :, None], picked, jnp.zeros_like(picked))
-    returned = lax.all_to_all(picked, "tok", split_axis=1, concat_axis=1, tiled=True)
+    devices = lax.axis_size("tok")
+    shards = jnp.stack(jnp.split(picked, devices, axis=1), axis=0)
+    shards = lax.all_to_all(shards, "tok", split_axis=0, concat_axis=0)
+    returned = jnp.concatenate(shards, axis=1)
     input_grad = jnp.take(returned, my_clusters, axis=1).reshape(share_rows, tok_rows).T
     return input_grad
 

time: 151 us -> 160 us (1.060)
  local copies, waits for them, and re-layouts: 9.34 us -> 19 us
    unnamed x14 -> x29, local copies, waits for them, and re-layouts: 1.48 us -> 10.6 us
where the time goes in v1:
time: 160 us; the launch traced here: 159 us
  waiting for transfers between devices  53.8 us (34%)
  blocking collectives  47.3 us (30%)
  local copies, waits for them, and re-layouts  19 us (12%)
  starting transfers between devices  14 us (9%)
  between operations  13.7 us (9%)
  matrix products  6.38 us (4%)
  other arithmetic  4.67 us (3%)
    all_to_all x1, blocking collectives, per_device(): lax.all_to_all(outgoing(keys), 'tok', split_axis=0, concat_axis=0, tiled=...  20.2 us
    all_to_all x1, blocking collectives, per_device(): lax.all_to_all(outgoing(grad_heads), 'tok', split_axis=0, concat_axis=0,...  18.4 us
    all_to_all x1, waiting for transfers between devices, per_device(): shards = lax.all_to_all(shards, 'tok', split_axis=0, concat_axis=0)  14.1 us
    reduce_scatter x1, waiting for transfers between devices, per_device(): lax.psum_scatter(total.astype(jnp.bfloat16), 'head', scatter_dimension=0,...  14.1 us
    all_to_all x1, waiting for transfers between devices, per_device(): lax.all_to_all(outgoing(values), 'tok', split_axis=0, concat_axis=0, tile...  13.4 us
    all_to_all x1, waiting for transfers between devices, per_device(): lax.all_to_all(outgoing(queries), 'tok', split_axis=0, concat_axis=0, til...  12.2 us
    unnamed x29, local copies, waits for them, and re-layouts  10.6 us
    all_gather x1, blocking collectives, per_device(): lax.all_gather(out_grad, 'head', axis=1, tiled=True)  8.79 us
  transfers between devices with their start and end apart: 4, of which 4 were waited for; matrix products, arithmetic and copies ran while one was open for 2% of the time, Pallas kernels for 0%

profile of v1, /device:TPU:0, one launch (start us, length us, event | category | flops | bytes accessed | tf_op | source)
XLA Modules:
  0.0 158.9 jit_solution(12673336185960434590)
XLA Ops:
  6.5 0.8 compare_and_fusion.3
  7.6 8.8 %all_gather.3 = bf16[192,1024]{1,0:T(8,128)(2,1)S(1)} all-gather(bf16[192,512]{1,0:T(8,128)(2,1)} %param.16), channel_id=1, replica_groups=mesh['head'=2,'tok'=16] {'head'}, dimensions={1}, use_global_device_ids=true | all-gather | bytes 589824 | tf_op jit(solution)/shard_map/all_gather | solution.py:22
  16.3 1.8 %convolution_convert_fusion.1 = bf16[192,512]{1,0:T(8,128)(2,1)S(1)} fusion(bf16[192,1024]{1,0:T(8,128)(2,1)S(1)} %all_gather.3, bf16[512,1024]{1,0:T(8,128)(2,1)} %param.20), kind=kOutput, calls=%fused_computation.25 | convolution fusion | flops 201424896 | bytes 1638400 | tf_op jit(solution)/shard_map/td,hd->th/dot_general | solution.py:20
  20.5 1.3 select_select_fusion.2
  21.8 20.2 %all_to_all.25 = bf16[16,32,512]{2,1,0:T(8,128)(2,1)S(1)} all-to-all(bf16[16,32,512]{2,1,0:T(8,128)(2,1)S(1)} %get-tuple-element.18), channel_id=1, replica_groups=mesh['head'=2,'tok'=16] {'tok'}, dimensions={0} | all-to-all | bytes 1048576 | tf_op jit(solution)/shard_map/all_to_all | solution.py:45
  42.0 18.4 %all_to_all.26 = bf16[16,32,512]{2,1,0:T(8,128)(2,1)S(1)} all-to-all(bf16[16,32,512]{2,1,0:T(8,128)(2,1)S(1)} %get-tuple-element.16), channel_id=1, replica_groups=mesh['head'=2,'tok'=16] {'tok'}, dimensions={0} | all-to-all | bytes 1048576 | tf_op jit(solution)/shard_map/all_to_all | solution.py:47
  60.4 4.2 %all-to-all-start.3 = ((bf16[16,32,512]{2,1,0:T(8,128)(2,1)}), bf16[16,32,512]{2,1,0:T(8,128)(2,1)S(1)}, u32[]{:S(2)}, u32[]{:S(2)}) async-start(bf16[16,32,512]{2,1,0:T(8,128)(2,1)} %get-tuple-element.17), calls=%async_computation.3 | async-start | bytes 1048576 | tf_op jit(solution)/shard_map/all_to_all | solution.py:46
  65.4 13.4 %all-to-all-done.3 = bf16[16,32,512]{2,1,0:T(8,128)(2,1)S(1)} async-done(((bf16[16,32,512]{2,1,0:T(8,128)(2,1)}), bf16[16,32,512]{2,1,0:T(8,128)(2,1)S(1)}, u32[]{:S(2)}, u32[]{:S(2)}) %all-to-all-start.3) | async-done | bytes 524320 | tf_op jit(solution)/shard_map/all_to_all | solution.py:46
  78.8 4.2 %all-to-all-start.1 = ((bf16[16,32,512]{2,1,0:T(8,128)(2,1)}), bf16[16,32,512]{2,1,0:T(8,128)(2,1)S(1)}, u32[]{:S(2)}, u32[]{:S(2)}) async-start(bf16[16,32,512]{2,1,0:T(8,128)(2,1)} %get-tuple-element.15), calls=%async_computation.1 | async-start | bytes 1048576 | tf_op jit(solution)/shard_map/all_to_all | solution.py:44
  85.1 12.2 %all-to-all-done.1 = bf16[16,32,512]{2,1,0:T(8,128)(2,1)S(1)} async-done(((bf16[16,32,512]{2,1,0:T(8,128)(2,1)}), bf16[16,32,512]{2,1,0:T(8,128)(2,1)S(1)}, u32[]{:S(2)}, u32[]{:S(2)}) %all-to-all-start.1) | async-done | bytes 524320 | tf_op jit(solution)/shard_map/all_to_all | solution.py:44
  98.9 0.6 fusion.39
  99.5 0.9 convolution_convert_fusion
  101.9 0.7 copy-done.4
  103.2 0.7 copy-done.5
  103.9 1.3 fusion.6
  105.4 14.1 %reduce-scatter.2.cloned.1.call-done = bf16[512,256]{0,1:T(8,128)(2,1)} async-done(((bf16[1024,256]{0,1:T(8,128)(2,1)}), bf16[512,256]{0,1:T(8,128)(2,1)}) %reduce-scatter.2.cloned.1.call-update) | async-done | bytes 262160 | tf_op jit(solution)/shard_map/reduce_scatter | solution.py:119
  119.5 1.5 gather_fusion
  121.2 0.6 fusion.29
  121.8 0.6 fusion.28
  123.0 0.6 fusion.26
  124.2 0.6 fusion.24
  125.4 0.6 fusion.22
  126.6 0.6 fusion.20
  127.2 0.6 fusion.19
  127.8 0.6 fusion.18
  128.4 0.6 fusion.17
  129.0 0.6 fusion.16
  129.7 0.6 fusion.15
  130.3 0.6 fusion.14
  130.9 5.6 %all-to-all-start.4 = ((bf16[16,512,1,32]{1,3,2,0:T(8,128)(2,1)}), bf16[16,512,1,32]{1,3,2,0:T(8,128)(2,1)S(1)}, u32[]{:S(2)}, u32[]{:S(2)}) async-start(bf16[16,512,1,32]{1,3,2,0:T(8,128)(2,1)} %fusion.14), calls=%async_computation.5 | async-start | bytes 1048576 | tf_op jit(solution)/shard_map/all_to_all | solution.py:127
  136.7 14.1 %all-to-all-done.4 = bf16[16,512,1,32]{1,3,2,0:T(8,128)(2,1)S(1)} async-done(((bf16[16,512,1,32]{1,3,2,0:T(8,128)(2,1)}), bf16[16,512,1,32]{1,3,2,0:T(8,128)(2,1)S(1)}, u32[]{:S(2)}, u32[]{:S(2)}) %all-to-all-start.4) | async-done | bytes 524320 | tf_op jit(solution)/shard_map/all_to_all | solution.py:127
  151.3 0.8 bitcast_select_fusion
  (71 shorter events, 12.4 us)
Async XLA Ops:
  6.5 94.9 %copy-start = (bf16[1024,512]{1,0:T(8,128)(2,1)S(1)}, bf16[1024,512]{1,0:T(8,128)(2,1)}, u32[]{:S(2)}) copy-start(bf16[1024,512]{1,0:T(8,128)(2,1)} %param.17) | copy-start | bytes 3145732
  16.3 2.4 %copy-start.1 = (bf16[192,512]{1,0:T(8,128)(2,1)S(1)}, bf16[192,512]{1,0:T(8,128)(2,1)}, u32[]{:S(2)}) copy-start(bf16[192,512]{1,0:T(8,128)(2,1)} %param.14) | copy-start | bytes 589828
  18.1 1.2 copy-start.2
  18.7 1.2 copy-start.3
  42.0 22.5 %copy-start.6 = (s32[96]{0:T(128)S(1)}, s32[96]{0:T(128)}, u32[]{:S(2)}) copy-start(s32[96]{0:T(128)} %param.21) | copy-start | bytes 1156
  60.4 18.4 %all-to-all-start.3 = ((bf16[16,32,512]{2,1,0:T(8,128)(2,1)}), bf16[16,32,512]{2,1,0:T(8,128)(2,1)S(1)}, u32[]{:S(2)}, u32[]{:S(2)}) async-start(bf16[16,32,512]{2,1,0:T(8,128)(2,1)} %get-tuple-element.17), calls=%async_computation.3 | async-start | bytes 1048576 | tf_op jit(solution)/shard_map/all_to_all | solution.py:46
  78.8 18.4 %all-to-all-start.1 = ((bf16[16,32,512]{2,1,0:T(8,128)(2,1)}), bf16[16,32,512]{2,1,0:T(8,128)(2,1)S(1)}, u32[]{:S(2)}, u32[]{:S(2)}) async-start(bf16[16,32,512]{2,1,0:T(8,128)(2,1)} %get-tuple-element.15), calls=%async_computation.1 | async-start | bytes 1048576 | tf_op jit(solution)/shard_map/all_to_all | solution.py:44
  83.0 36.5 %reduce-scatter.2.cloned.1.call-start = ((), (), s32[]{:S(2)}) async-start(), calls=%async_computation.6 | async-start | bytes 786432 | tf_op jit(solution)/shard_map/reduce_scatter | solution.py:119
  101.4 1.2 copy-start.4
  102.7 1.2 copy-start.5
  130.9 19.9 %all-to-all-start.4 = ((bf16[16,512,1,32]{1,3,2,0:T(8,128)(2,1)}), bf16[16,512,1,32]{1,3,2,0:T(8,128)(2,1)S(1)}, u32[]{:S(2)}, u32[]{:S(2)}) async-start(bf16[16,512,1,32]{1,3,2,0:T(8,128)(2,1)} %fusion.14), calls=%async_computation.5 | async-start | bytes 1048576 | tf_op jit(solution)/shard_map/all_to_all | solution.py:127
Sparse Core Ops, SparseCore 0:
  105.3 14.1 reduce-scatter.1
